TPU v7x, 32 devices: a whole 2x2x4 slice. The times are simulated.
32 devices in a mesh: groups: 2 (over y), tile: 4 (over z), tm: 4 (over x, core).
Axes of the slice: x: 2, y: 2, z: 4, core: 2. Of those that a mesh axis runs over, the one named last changes fastest.
Arguments:
- hidden: bfloat16 [8, 16, 3072], P(('groups', 'tm'), 'tile'), parts along dimension 0, may hold values from -12 to 12
- modulation: float32 [4, 3072], P('groups'), parts along dimension 0, may hold values from -2.5 to 2.5
- proj_weight: bfloat16 [3072, 64], replicated, may hold values from -0.109375 to 0.109375
- conv_in_weight: bfloat16 [3, 3, 3, 16, 256], replicated, may hold values from -0.3125 to 0.3125
- up_weight: bfloat16 [3, 3, 3, 256, 256], replicated, may hold values from -0.15625 to 0.15625
Outputs:
- decoded: bfloat16 [8, 16, 16, 256], P(('groups', 'tm'), None, 'tile'), parts along dimension 0
There are 2 independent parts, one for each index of `groups`. A program takes and returns all parts, laid end to end along the dimension named above; an argument that names none is the same for every part. Nothing has to cross between parts.
All inputs are finite; a program needn't handle non-finite values.
Results may differ from a plain program's by a relative error of at most 0.0065.
Values may be sent and summed in bfloat16 or wider, within the bound.
A program may use at most 64 MiB of HBM per device.

v0:
```python
import functools

import jax
import jax.numpy as jnp
from jax import lax
from jax.experimental import pallas as pl
from jax.experimental.pallas import tpu as pltpu
from jax.sharding import PartitionSpec as P

REACH = 5
EDGE = 8
UP_CHUNKS = 9
MESH = pl.DeviceIdType.MESH


def fused_kernel(
    n_tile,
    n_tm,
    hidden_hbm,
    mod_hbm,
    proj_hbm,
    cin_hbm,
    up_hbm,
    out_ref,
    hid,
    mod,
    proj,
    cin,
    upw,
    pad_p,
    outbox,
    inbox,
    lat,
    feat,
    pairs,
    joined,
    load_sem,
    up_sem,
    send_sem,
    recv_sem,
    own_sem,
):
    tile = lax.axis_index("tile")
    frame = lax.axis_index("tm")
    rows = 2 * n_tile
    first = jnp.maximum(frame - (REACH - 1), 0)
    after = jnp.minimum(frame + REACH, n_tm)

    barrier = pltpu.get_barrier_semaphore()

    def greet_frame(source, _):
        def greet(column, _):
            @pl.when(jnp.logical_or(source != frame, column != tile))
            def _():
                pl.semaphore_signal(
                    barrier,
                    inc=1,
                    device_id={"tile": column, "tm": source},
                    device_id_type=MESH,
                )

            return 0

        return lax.fori_loop(0, n_tile, greet, 0)

    lax.fori_loop(first, frame + 1, greet_frame, 0)

    loads = [
        pltpu.make_async_copy(hidden_hbm.at[0], hid, load_sem.at[0]),
        pltpu.make_async_copy(mod_hbm, mod, load_sem.at[1]),
        pltpu.make_async_copy(proj_hbm, proj, load_sem.at[2]),
    ]
    load_cin = pltpu.make_async_copy(cin_hbm, cin.at[:, pl.ds(0, 48), :], load_sem.at[3])
    per_chunk = 27 // UP_CHUNKS
    load_up = [
        pltpu.make_async_copy(
            up_hbm.at[pl.ds(n * per_chunk, per_chunk)],
            upw.at[pl.ds(n * per_chunk, per_chunk)],
            up_sem.at[n],
        )
        for n in range(UP_CHUNKS)
    ]
    for copy in loads + [load_cin] + load_up:
        copy.start()

    cin[:, 48:, :] = jnp.zeros((9, 80, 256), jnp.bfloat16)
    pad_p[...] = jnp.zeros_like(pad_p)
    for k in range(4):
        for slot in range(REACH):
            lat[k, slot, 0:EDGE, :] = jnp.zeros((EDGE, 128), jnp.float32)
            lat[k, slot, EDGE + rows :, :] = jnp.zeros((EDGE, 128), jnp.float32)
        for t in range(3):
            feat[k, t, 0:EDGE, :] = jnp.zeros((EDGE, 256), jnp.float32)
            feat[k, t, EDGE + rows :, :] = jnp.zeros((EDGE, 256), jnp.float32)

    loads[0].wait()
    values = hid[...].astype(jnp.float32)
    width = values.shape[-1]
    mean = jnp.sum(values, axis=-1, keepdims=True) * (1.0 / width)
    centred = values - mean
    var = jnp.sum(centred * centred, axis=-1, keepdims=True) * (1.0 / width)
    normed = centred * lax.rsqrt(var + 1e-06)
    loads[1].wait()
    modulated = (normed * (1.0 + mod[1:2, :]) + mod[0:1, :]).astype(jnp.bfloat16)
    loads[2].wait()
    patches = lax.dot_general(
        modulated, proj[...], (((1,), (1,)), ((), ())), preferred_element_type=jnp.float32
    )
    pad_p[0:n_tile, 0:64] = patches.astype(jnp.bfloat16).astype(jnp.float32)

    padded = pad_p[...]
    height = padded.shape[0]
    lanes = lax.broadcasted_iota(jnp.int32, padded.shape, 1)
    for i in range(2):
        own = padded if i == 0 else pltpu.roll(padded, 96, 1)
        own = jnp.where(lanes < 32, own, 0.0)
        window = (
            pltpu.roll(own, 1, 0)
            + pltpu.roll(own, 32, 1)
            + pltpu.roll(pltpu.roll(own, height - 1, 0), 64, 1)
        )
        for column in range(n_tile):
            outbox[column, i : i + 1, :] = window[column : column + 1, :]

    own_copy = pltpu.make_async_copy(outbox.at[tile], inbox.at[0, tile], own_sem)
    own_copy.start()
    pl.semaphore_wait(barrier, (after - frame) * n_tile - 1)

    for d in range(REACH):

        @pl.when(frame + d < n_tm)
        def _(d=d):
            def send(step, _):
                column = lax.rem(tile + step, n_tile)
                pltpu.make_async_remote_copy(
                    src_ref=outbox.at[column],
                    dst_ref=inbox.at[d, tile],
                    send_sem=send_sem.at[d],
                    recv_sem=recv_sem.at[d],
                    device_id={"tile": column, "tm": frame + d},
                    device_id_type=MESH,
                ).start()
                return 0

            lax.fori_loop(1 if d == 0 else 0, n_tile, send, 0)

    own_copy.wait()
    for d in range(REACH):
        count = n_tile - 1 if d == 0 else n_tile

        @pl.when(frame - d >= 0)
        def _(d=d, count=count):
            arrived = inbox.at[d, pl.ds(0, count)]
            pltpu.make_async_copy(arrived, arrived, recv_sem.at[d]).wait()

    for slot in range(REACH):
        distance = jnp.minimum(REACH - 1 - slot, frame)
        for r in range(n_tile):
            lat[0, slot, EDGE + 2 * r : EDGE + 2 * r + 2, :] = inbox[distance, r]
        field = lat[0, slot, EDGE : EDGE + rows, :]
        for k in range(1, 4):
            lat[k, slot, EDGE : EDGE + rows, :] = pltpu.roll(field, 128 - 16 * k, 1)

    load_cin.wait()
    taps = []
    for a in range(3):
        for b in range(3):
            start = EDGE - 1 + b
            taps.append(
                jnp.concatenate(
                    [
                        lat[k, t + a, start : start + rows, :]
                        for k in range(4)
                        for t in range(3)
                    ],
                    axis=0,
                ).astype(jnp.bfloat16)
            )
    summed = jnp.dot(
        jnp.concatenate(taps, axis=1),
        cin[...].reshape(9 * 128, 256),
        preferred_element_type=jnp.float32,
    )
    features = (summed / (1.0 + jnp.exp(-summed))).astype(jnp.bfloat16).astype(jnp.float32)
    for k in range(4):
        column = 2 * tile - 1 + k
        inside = jnp.logical_and(column >= 0, column < 2 * n_tile)
        for t in range(3):
            block = features[(3 * k + t) * rows : (3 * k + t + 1) * rows]
            if k in (0, 3):
                block = jnp.where(inside, block, 0.0)
            feat[k, t, EDGE : EDGE + rows, :] = block

    for tap_y in range(3):
        for t in range(3):
            for k in range(4):
                pairs[tap_y, t, k] = jnp.concatenate(
                    [
                        feat[k, t, EDGE + (p + tap_y - 1) // 2 : EDGE + (p + tap_y - 1) // 2 + rows, :]
                        for p in range(2)
                    ],
                    axis=0,
                ).astype(jnp.bfloat16)

    total = None
    for t in range(3):
        for tap_y in range(3):
            for tap_x in range(3):
                tap = (3 * t + tap_y) * 3 + tap_x
                if tap % per_chunk == 0:
                    load_up[tap // per_chunk].wait()
                left = jnp.concatenate(
                    [pairs[tap_y, t, (x + tap_x - 1) // 2 + 1] for x in range(4)], axis=0
                )
                part = jnp.dot(left, upw[tap], preferred_element_type=jnp.float32)
                total = part if total is None else total + part

    for x in range(4):
        for p in range(2):
            at = (2 * x + p) * rows
            for half in range(2):
                joined[half, pl.ds(4 * p + x, rows, stride=8), :] = total[
                    at : at + rows, 128 * half : 128 * (half + 1)
                ]
    for row in range(2 * rows):
        for half in range(2):
            out_ref[0, row, :, 128 * half : 128 * (half + 1)] = joined[
                half, 4 * row : 4 * row + 4, :
            ].astype(jnp.bfloat16)

    for d in range(REACH):
        count = n_tile - 1 if d == 0 else n_tile

        @pl.when(frame + d < n_tm)
        def _(d=d, count=count):
            left = outbox.at[pl.ds(0, count)]
            pltpu.make_async_copy(left, left, send_sem.at[d]).wait()


def on_device(n_tile, n_tm, hidden, modulation, proj_weight, conv_in_weight, up_weight):
    frames_dev, tokens, width = hidden.shape
    lat_ch, channels = conv_in_weight.shape[3:]
    assert frames_dev == 1 and tokens == n_tile and lat_ch == 16 and channels == 256
    rows = 2 * n_tile
    field = rows + 2 * EDGE
    hbm = pl.BlockSpec(memory_space=pltpu.HBM)
    return pl.pallas_call(
        functools.partial(fused_kernel, n_tile, n_tm),
        out_shape=jax.ShapeDtypeStruct((1, 2 * rows, 4, channels), jnp.bfloat16),
        in_specs=[hbm] * 5,
        out_specs=pl.BlockSpec(memory_space=pltpu.VMEM),
        scratch_shapes=[
            pltpu.VMEM((tokens, width), jnp.bfloat16),
            pltpu.VMEM((2, width), jnp.float32),
            pltpu.VMEM((4 * lat_ch, width), jnp.bfloat16),
            pltpu.VMEM((9, 128, channels), jnp.bfloat16),
            pltpu.VMEM((27, channels, channels), jnp.bfloat16),
            pltpu.VMEM(((tokens // 8 + 1) * 8, 128), jnp.float32),
            pltpu.VMEM((n_tile, 2, 128), jnp.float32),
            pltpu.VMEM((REACH, n_tile, 2, 128), jnp.float32),
            pltpu.VMEM((4, REACH, field, 128), jnp.float32),
            pltpu.VMEM((4, 3, field, channels), jnp.float32),
            pltpu.VMEM((3, 3, 4, 2 * rows, channels), jnp.bfloat16),
            pltpu.VMEM((2, 8 * rows, 128), jnp.float32),
            pltpu.SemaphoreType.DMA((4,)),
            pltpu.SemaphoreType.DMA((UP_CHUNKS,)),
            pltpu.SemaphoreType.DMA((REACH,)),
            pltpu.SemaphoreType.DMA((REACH,)),
            pltpu.SemaphoreType.DMA,
        ],
        compiler_params=pltpu.CompilerParams(
            collective_id=0, has_side_effects=True
        ),
    )(
        hidden,
        modulation,
        proj_weight.T,
        conv_in_weight.reshape(9, 48, channels),
        up_weight.reshape(27, channels, channels),
    )


def solution(mesh):
    in_specs = (P(("groups", "tm"), "tile", None), P("groups", None), P(), P(), P())
    out_specs = P(("groups", "tm"), None, "tile", None)
    body = functools.partial(on_device, mesh.shape["tile"], mesh.shape["tm"])
    return jax.shard_map(
        body, mesh=mesh, in_specs=in_specs, out_specs=out_specs, check_vma=False
    )
```

profile of v0, /device:TPU:0, one launch (start us, length us, event | category | flops | bytes accessed | tf_op | source)
XLA Modules:
  0.0 12.8 jit_solution(16366375362219759552)
XLA Ops:
  0.0 11.4 %shard_map.55 = bf16[1,16,4,256]{3,2,1,0:T(4,128)(2,1)} custom-call(bf16[1,4,3072]{2,1,0:T(4,128)(2,1)} %hidden_hbm.1, f32[2,3072]{1,0:T(2,128)} %mod_hbm.1, bf16[64,3072]{1,0:T(8,128)(2,1)} %bitcast.4, bf16[9,48,256]{2,1,0:T(8,128)(2,1)} %bitcast.5, bf16[27,256,256]{2,1,0:T(8,128)(2,1)} %bitcast.3), custom_call_target="tpu_custom_call" | custom-call | tf_op jit(solution)/shard_map/pallas_call | solution.py:247
  11.4 1.4 %copy.7 = bf16[1,16,4,256]{3,2,1,0:T(4,128)(2,1)} copy(bf16[1,16,4,256]{3,2,1,0:T(4,128)(2,1)} %shard_map.55) | data formatting | bytes 65536
where the time goes:
time: 13 us; the launch traced here: 12.8 us
  Pallas kernels  11.4 us (88%)
  local copies, waits for them, and re-layouts  1.39 us (11%)
    pallas_call x1, Pallas kernels, on_device(): pl.pallas_call(functools.partial(fused_kernel, n_tile, n_tm), out_shape=j...  11.4 us
    unnamed x1, local copies, waits for them, and re-layouts  1.39 us

commit v1 on v0

--- a/solution.py
+++ b/solution.py
@@ -246,7 +246,7 @@
     hbm = pl.BlockSpec(memory_space=pltpu.HBM)
     return pl.pallas_call(
         functools.partial(fused_kernel, n_tile, n_tm),
-        out_shape=jax.ShapeDtypeStruct((1, 2 * rows, 4, channels), jnp.bfloat16),
+        out_shape=pltpu.VMEM((1, 2 * rows, 4, channels), jnp.bfloat16),
         in_specs=[hbm] * 5,
         out_specs=pl.BlockSpec(memory_space=pltpu.VMEM),
         scratch_shapes=[

time: 13 us -> 11.6 us (0.89)
  local copies, waits for them, and re-layouts: 1.39 us -> 0.62 us
  Pallas kernels: 11.4 us -> 10.8 us
    unnamed x1, local copies, waits for them, and re-layouts: 1.39 us -> 0.62 us
    pallas_call x1, Pallas kernels: 11.4 us -> 10.8 us  [on_device(): pl.pallas_call(functools.partial(fused_kernel, n_tile, n_tm), out_shape=p...]
where the time goes in v1:
time: 11.6 us; the launch traced here: 11.4 us
  Pallas kernels  10.8 us (93%)
  local copies, waits for them, and re-layouts  0.62 us (5%)
    pallas_call x1, Pallas kernels, on_device(): pl.pallas_call(functools.partial(fused_kernel, n_tile, n_tm), out_shape=p...  10.8 us
    unnamed x1, local copies, waits for them, and re-layouts  0.62 us

profile of v1, /device:TPU:0, one launch (start us, length us, event | category | flops | bytes accessed | tf_op | source)
XLA Modules:
  0.0 11.4 jit_solution(18341288943180664302)
XLA Ops:
  0.0 10.8 %shard_map.55 = bf16[1,16,4,256]{3,2,1,0:T(4,128)(2,1)S(1)} custom-call(bf16[1,4,3072]{2,1,0:T(4,128)(2,1)} %hidden_hbm.1, f32[2,3072]{1,0:T(2,128)} %mod_hbm.1, bf16[64,3072]{1,0:T(8,128)(2,1)} %bitcast.4, bf16[9,48,256]{2,1,0:T(8,128)(2,1)} %bitcast.5, bf16[27,256,256]{2,1,0:T(8,128)(2,1)} %bitcast.3), custom_call_target="tpu_custom_call" | custom-call | tf_op jit(solution)/shard_map/pallas_call | solution.py:247
  10.8 0.6 %copy.7 = bf16[1,16,4,256]{3,2,1,0:T(4,128)(2,1)} copy(bf16[1,16,4,256]{3,2,1,0:T(4,128)(2,1)S(1)} %shard_map.55) | data formatting | bytes 65536

commit v2 on v1

--- a/solution.py
+++ b/solution.py
@@ -9,7 +9,7 @@
 
 REACH = 5
 EDGE = 8
-UP_CHUNKS = 9
+UP_CHUNKS = 3
 MESH = pl.DeviceIdType.MESH
 
 
@@ -80,7 +80,7 @@
         )
         for n in range(UP_CHUNKS)
     ]
-    for copy in loads + [load_cin] + load_up:
+    for copy in loads:
         copy.start()
 
     cin[:, 48:, :] = jnp.zeros((9, 80, 256), jnp.bfloat16)
@@ -103,6 +103,8 @@
     loads[1].wait()
     modulated = (normed * (1.0 + mod[1:2, :]) + mod[0:1, :]).astype(jnp.bfloat16)
     loads[2].wait()
+    for copy in [load_cin] + load_up:
+        copy.start()
     patches = lax.dot_general(
         modulated, proj[...], (((1,), (1,)), ((), ())), preferred_element_type=jnp.float32
     )
@@ -204,16 +206,20 @@
 
     total = None
     for t in range(3):
-        for tap_y in range(3):
-            for tap_x in range(3):
-                tap = (3 * t + tap_y) * 3 + tap_x
-                if tap % per_chunk == 0:
-                    load_up[tap // per_chunk].wait()
-                left = jnp.concatenate(
+        load_up[t].wait()
+        left = jnp.concatenate(
+            [
+                jnp.concatenate(
                     [pairs[tap_y, t, (x + tap_x - 1) // 2 + 1] for x in range(4)], axis=0
                 )
-                part = jnp.dot(left, upw[tap], preferred_element_type=jnp.float32)
-                total = part if total is None else total + part
+                for tap_y in range(3)
+                for tap_x in range(3)
+            ],
+            axis=1,
+        )
+        right = upw[9 * t : 9 * t + 9].reshape(9 * 256, 256)
+        part = jnp.dot(left, right, preferred_element_type=jnp.float32)
+        total = part if total is None else total + part
 
     for x in range(4):
         for p in range(2):

time: 11.6 us -> 10.5 us (0.905)
  Pallas kernels: 10.8 us -> 9.69 us
    pallas_call x1, Pallas kernels: 10.8 us -> 9.69 us  [on_device(): pl.pallas_call(functools.partial(fused_kernel, n_tile, n_tm), out_shape=p...]
where the time goes in v2:
time: 10.5 us; the launch traced here: 10.3 us
  Pallas kernels  9.69 us (92%)
  local copies, waits for them, and re-layouts  0.62 us (6%)
    pallas_call x1, Pallas kernels, on_device(): pl.pallas_call(functools.partial(fused_kernel, n_tile, n_tm), out_shape=p...  9.69 us
    unnamed x1, local copies, waits for them, and re-layouts  0.62 us

profile of v2, /device:TPU:0, one launch (start us, length us, event | category | flops | bytes accessed | tf_op | source)
XLA Modules:
  0.0 10.3 jit_solution(12247797746657470796)
XLA Ops:
  0.0 9.7 %shard_map.55 = bf16[1,16,4,256]{3,2,1,0:T(4,128)(2,1)S(1)} custom-call(bf16[1,4,3072]{2,1,0:T(4,128)(2,1)} %hidden_hbm.1, f32[2,3072]{1,0:T(2,128)} %mod_hbm.1, bf16[64,3072]{1,0:T(8,128)(2,1)} %bitcast.4, bf16[9,48,256]{2,1,0:T(8,128)(2,1)} %bitcast.5, bf16[27,256,256]{2,1,0:T(8,128)(2,1)} %bitcast.3), custom_call_target="tpu_custom_call" | custom-call | tf_op jit(solution)/shard_map/pallas_call | solution.py:253
  9.7 0.6 %copy.7 = bf16[1,16,4,256]{3,2,1,0:T(4,128)(2,1)} copy(bf16[1,16,4,256]{3,2,1,0:T(4,128)(2,1)S(1)} %shard_map.55) | data formatting | bytes 65536

commit v3 on v2

--- a/solution.py
+++ b/solution.py
@@ -204,22 +204,22 @@
                     axis=0,
                 ).astype(jnp.bfloat16)
 
-    total = None
     for t in range(3):
         load_up[t].wait()
-        left = jnp.concatenate(
-            [
-                jnp.concatenate(
-                    [pairs[tap_y, t, (x + tap_x - 1) // 2 + 1] for x in range(4)], axis=0
-                )
-                for tap_y in range(3)
-                for tap_x in range(3)
-            ],
-            axis=1,
-        )
-        right = upw[9 * t : 9 * t + 9].reshape(9 * 256, 256)
-        part = jnp.dot(left, right, preferred_element_type=jnp.float32)
-        total = part if total is None else total + part
+    left = jnp.concatenate(
+        [
+            jnp.concatenate(
+                [pairs[tap_y, t, (x + tap_x - 1) // 2 + 1] for x in range(4)], axis=0
+            )
+            for t in range(3)
+            for tap_y in range(3)
+            for tap_x in range(3)
+        ],
+        axis=1,
+    )
+    total = jnp.dot(
+        left, upw[...].reshape(27 * 256, 256), preferred_element_type=jnp.float32
+    )
 
     for x in range(4):
         for p in range(2):

time: 10.5 us -> 10.4 us (level)
  no operation moved by 1% of the time
where the time goes in v3:
time: 10.4 us; the launch traced here: 10.2 us
  Pallas kernels  9.6 us (92%)
  local copies, waits for them, and re-layouts  0.62 us (6%)
    pallas_call x1, Pallas kernels, on_device(): pl.pallas_call(functools.partial(fused_kernel, n_tile, n_tm), out_shape=p...  9.6 us
    unnamed x1, local copies, waits for them, and re-layouts  0.62 us

profile of v3, /device:TPU:0, one launch (start us, length us, event | category | flops | bytes accessed | tf_op | source)
XLA Modules:
  0.0 10.2 jit_solution(17228790968889260745)
XLA Ops:
  0.0 9.6 %shard_map.55 = bf16[1,16,4,256]{3,2,1,0:T(4,128)(2,1)S(1)} custom-call(bf16[1,4,3072]{2,1,0:T(4,128)(2,1)} %hidden_hbm.1, f32[2,3072]{1,0:T(2,128)} %mod_hbm.1, bf16[64,3072]{1,0:T(8,128)(2,1)} %bitcast.4, bf16[9,48,256]{2,1,0:T(8,128)(2,1)} %bitcast.5, bf16[27,256,256]{2,1,0:T(8,128)(2,1)} %bitcast.3), custom_call_target="tpu_custom_call" | custom-call | tf_op jit(solution)/shard_map/pallas_call | solution.py:253
  9.6 0.6 %copy.7 = bf16[1,16,4,256]{3,2,1,0:T(4,128)(2,1)} copy(bf16[1,16,4,256]{3,2,1,0:T(4,128)(2,1)S(1)} %shard_map.55) | data formatting | bytes 65536
